TPU v7x, 32 devices: a whole 2x2x4 slice. The times are simulated.
32 devices in a mesh: dom: 16 (over z, x, core), mem: 2 (over y).
Axes of the slice: x: 2, y: 2, z: 4, core: 2. Of those that a mesh axis runs over, the one named last changes fastest.
Arguments:
- ensemble: bfloat16 [12, 32, 65536], P('mem', None, 'dom'), may hold values from -6 to 6
- observed: float32 [32, 16384], P(None, 'dom'), may hold values from -6 to 6
- tile_weight: bfloat16 [1536, 128, 128], P('dom')
- tile_block: int32 [1536], P('dom'), may hold values from 0 to 31
- tile_target: int32 [1536], P('dom'), may hold values from 0 to 127, as said below
- tile_count: int32 [16], P('dom'), may hold values from 48 to 96, as said below
Outputs:
- crps: float32 [32, 16384], P(None, 'dom')
Inputs may be any that keep to these rules, and one draw needn't show every extreme that they name: `tile_block`: a slot's source block, counted within its partition's cells. `tile_target`: slot k belongs to partition p = k // 96; its target tile is owned by one of the partitions p - 4 to p + 4, where partition o owns the 8 target tiles from o * 8 on. The live slots of partition p are the first tile_count[p] of its list; the rest are padding.
All inputs are finite; a program needn't handle non-finite values.
Results may differ from a plain program's by a relative error of at most 0.0003.
Values sent between devices are 32-bit elements; how exact they have to be, the bound alone decides.
A program may use at most 64 MiB of HBM per device.

v0:
```python
import math
import jax
import jax.numpy as jnp
from jax import lax
from jax.sharding import PartitionSpec as P

REACH = 4


def from_behind(value, axis, steps):
    count = lax.axis_size(axis)
    first, last = (max(0, -steps), min(count, count - steps))
    return lax.ppermute(value, axis, [(source, source + steps) for source in range(first, last)])


def pair_total(left_set, right_set):
    flat_left = left_set.reshape(left_set.shape[0], -1)
    flat_right = right_set.reshape(right_set.shape[0], -1)
    total_columns = flat_left.shape[1]
    block_span = math.gcd(total_columns, 1024)

    def block_pairs(first_column):
        left_cols = lax.dynamic_slice_in_dim(flat_left, first_column, block_span, 1)
        right_cols = lax.dynamic_slice_in_dim(flat_right, first_column, block_span, 1)
        return jnp.sum(jnp.abs(left_cols[:, None, :] - right_cols[None, :, :]), axis=(0, 1))

    column_starts = jnp.arange(total_columns // block_span, dtype=jnp.int32) * block_span
    return lax.map(block_pairs, column_starts).reshape(left_set.shape[1:])


def on_device(ensemble, observed, tile_weight, tile_block, tile_target, tile_count):
    groups, levels, src_cells = ensemble.shape
    block_cells = tile_weight.shape[1]
    channels = groups * levels
    tile_slots = tile_block.shape[0]
    values = ensemble.reshape(channels, src_cells // block_cells, block_cells)
    picked = jnp.take(values, tile_block, axis=1)
    partial_value = jnp.einsum(
        "csi,sij->scj", picked, tile_weight, preferred_element_type=jnp.float32
    )
    owned = observed.shape[1] // block_cells
    window = 2 * REACH + 1
    device = lax.axis_index("dom")
    local_tile = tile_target - (device - REACH) * owned
    rows_index = jnp.arange(window * owned, dtype=jnp.int32)
    is_live = jnp.arange(tile_slots, dtype=jnp.int32) < tile_count[0]
    chooser = ((rows_index[:, None] == local_tile[None, :]) & is_live[None, :]).astype(jnp.float32)
    owner_parts = jnp.dot(
        chooser,
        partial_value.reshape(tile_slots, channels * block_cells),
        precision=lax.Precision.HIGHEST,
        preferred_element_type=jnp.float32,
    )
    owner_parts = owner_parts.reshape(window, owned, channels * block_cells)
    summed = owner_parts[REACH]
    for offset in range(-REACH, REACH + 1):
        if offset != 0:
            summed = summed + from_behind(owner_parts[REACH + offset], "dom", offset)
    remapped = (
        summed.reshape(owned, groups, levels, block_cells)
        .transpose(1, 2, 0, 3)
        .reshape(groups, levels, owned * block_cells)
    )
    members = groups * lax.axis_size("mem")
    norm_pairs = 2.0 * members * (members - 1)
    regrouped = lax.all_to_all(remapped, "mem", split_axis=2, concat_axis=0, tiled=True)
    part_cells = regrouped.shape[2]
    observed_part = lax.dynamic_slice_in_dim(
        observed, lax.axis_index("mem") * part_cells, part_cells, 1
    )
    skill_sum = jnp.sum(jnp.abs(regrouped - observed_part[None]), axis=0)
    spread = pair_total(regrouped, regrouped)
    score_part = skill_sum / members - spread / norm_pairs
    return lax.all_gather(score_part, "mem", axis=1, tiled=True)


def solution(mesh):
    return jax.shard_map(
        on_device,
        mesh=mesh,
        in_specs=(
            P("mem", None, "dom"),
            P(None, "dom"),
            P("dom", None, None),
            P("dom"),
            P("dom"),
            P("dom"),
        ),
        out_specs=P(None, "dom"),
        check_vma=False,
    )
```

profile of v0, /device:TPU:1, one launch (start us, length us, event | category | flops | bytes accessed | tf_op | source)
XLA Modules:
  0.0 215.5 jit_solution(2916523083471834512)
XLA Ops:
  0.0 0.8 compare_select_fusion
  0.8 0.8 compare_and_fusion
  1.6 1.7 copy.18
  3.4 1.8 copy.13
  5.9 4.8 %gather_fusion = bf16[96,192,128]{2,1,0:T(8,128)(2,1)} fusion(bf16[192,32,128]{2,0,1:T(8,128)(2,1)} %copy.13, s32[1024]{0:T(1024)S(1)} %pad_clamp_fusion), kind=kCustom, calls=%fused_computation | custom fusion | bytes 9437568 | tf_op jit(solution)/shard_map/jit(_take)/gather | solution.py:37
  10.7 3.4 %fusion.3 = f32[96,192,128]{2,1,0:T(8,128)S(1)} fusion(bf16[96,128,128]{2,1,0:T(8,128)(2,1)S(1)} %copy-done, bf16[96,192,128]{2,1,0:T(8,128)(2,1)} %gather_fusion, pred[96]{0:T(512)(128)(4,1)S(1)} %compare_and_fusion), kind=kOutput, calls=%fused_computation.6 | convolution fusion | flops 606339072 | bytes 17301600 | tf_op jit(solution)/shard_map/csi,sij->scj/dot_general | solution.py:38
  14.1 10.0 %fusion = f32[72,24576]{1,0:T(8,128)S(1)} fusion(f32[12,8,192,128]{3,2,1,0:T(8,128)S(1)} %bitcast.32, s32[96]{0:T(128)S(1)} %broadcast_subtract_fusion, pred[96]{0:T(512)(128)(4,1)S(1)} %iota_compare_fusion.1), kind=kOutput, calls=%fused_computation.3 | convolution fusion | flops 2038445568 | bytes 16515552 | tf_op jit(solution)/shard_map/dot_general | solution.py:48
  24.5 1.3 collective-permute-start
  25.8 1.3 collective-permute-start.1
  27.1 1.3 collective-permute-start.2
  28.4 1.9 collective-permute-start.3
  30.4 5.1 %collective-permute-start.4 = (f32[8,24576]{1,0:T(8,128)S(1)}, f32[8,24576]{1,0:T(8,128)S(1)}, u32[]{:S(2)}, u32[]{:S(2)}) collective-permute-start(f32[8,24576]{1,0:T(8,128)S(1)} %get-tuple-element.54), channel_id=1, source_target_pairs={{0,2},{2,4},{4,6},{6,8},{8,10},{10,12},{12,14},{14,16},{16,18},{18... | collective-permute-start | bytes 2359304 | tf_op jit(solution)/shard_map/ppermute | solution.py:13
  35.5 10.3 %collective-permute-done = f32[8,24576]{1,0:T(8,128)S(1)} collective-permute-done((f32[8,24576]{1,0:T(8,128)S(1)}, f32[8,24576]{1,0:T(8,128)S(1)}, u32[]{:S(2)}, u32[]{:S(2)}) %collective-permute-start) | collective-permute-done | bytes 786464 | tf_op jit(solution)/shard_map/ppermute | solution.py:13
  45.8 3.0 %collective-permute-start.5 = (f32[8,24576]{1,0:T(8,128)S(1)}, f32[8,24576]{1,0:T(8,128)S(1)}, u32[]{:S(2)}, u32[]{:S(2)}) collective-permute-start(f32[8,24576]{1,0:T(8,128)S(1)} %get-tuple-element.53), channel_id=1, source_target_pairs={{0,4},{2,6},{4,8},{6,10},{8,12},{10,14},{12,16},{14,18},{16,20},{1... | collective-permute-start | bytes 2359304 | tf_op jit(solution)/shard_map/ppermute | solution.py:13
  48.8 15.2 %collective-permute-done.1 = f32[8,24576]{1,0:T(8,128)S(1)} collective-permute-done((f32[8,24576]{1,0:T(8,128)S(1)}, f32[8,24576]{1,0:T(8,128)S(1)}, u32[]{:S(2)}, u32[]{:S(2)}) %collective-permute-start.1) | collective-permute-done | bytes 786464 | tf_op jit(solution)/shard_map/ppermute | solution.py:13
  64.1 12.9 %collective-permute-start.6 = (f32[8,24576]{1,0:T(8,128)S(1)}, f32[8,24576]{1,0:T(8,128)S(1)}, u32[]{:S(2)}, u32[]{:S(2)}) collective-permute-start(f32[8,24576]{1,0:T(8,128)S(1)} %get-tuple-element.52), channel_id=1, source_target_pairs={{0,6},{2,8},{4,10},{6,12},{8,14},{10,16},{12,18},{14,20},{16,22},{... | collective-permute-start | bytes 2359304 | tf_op jit(solution)/shard_map/ppermute | solution.py:13
  77.0 23.6 %collective-permute-start.7 = (f32[8,24576]{1,0:T(8,128)S(1)}, f32[8,24576]{1,0:T(8,128)S(1)}, u32[]{:S(2)}, u32[]{:S(2)}) collective-permute-start(f32[8,24576]{1,0:T(8,128)S(1)} %get-tuple-element.51), channel_id=1, source_target_pairs={{0,8},{2,10},{4,12},{6,14},{8,16},{10,18},{12,20},{14,22},{16,24},... | collective-permute-start | bytes 2359304 | tf_op jit(solution)/shard_map/ppermute | solution.py:13
  100.6 8.8 %collective-permute-done.7 = f32[8,24576]{1,0:T(8,128)S(1)} collective-permute-done((f32[8,24576]{1,0:T(8,128)S(1)}, f32[8,24576]{1,0:T(8,128)S(1)}, u32[]{:S(2)}, u32[]{:S(2)}) %collective-permute-start.7) | collective-permute-done | bytes 786464 | tf_op jit(solution)/shard_map/ppermute | solution.py:13
  109.5 1.2 fusion.14
  110.7 4.3 %copy.14 = f32[6,32,8,128]{1,0,3,2:T(8,128)} copy(f32[6,32,8,128]{3,2,1,0:T(8,128)} %bitcast.39) | data formatting | bytes 1572864 | tf_op jit(solution)/shard_map/transpose | solution.py:61
  114.9 4.0 %reshape.66 = f32[2,1,98304]{2,1,0:T(1,128)} reshape(f32[1024,6,32]{2,1,0:T(8,128)} %bitcast.33) | data formatting | bytes 1572864
  119.0 4.3 %all-to-all-start = ((f32[2,1,98304]{2,1,0:T(1,128)}), f32[2,1,98304]{2,1,0:T(1,128)}, u32[]{:S(2)}, u32[]{:S(2)}) async-start(f32[2,1,98304]{2,1,0:T(1,128)} %reshape.66), calls=%async_computation | async-start | bytes 1572864 | tf_op jit(solution)/shard_map/all_to_all | solution.py:66
  123.3 8.5 %all-to-all-done = f32[2,1,98304]{2,1,0:T(1,128)} async-done(((f32[2,1,98304]{2,1,0:T(1,128)}), f32[2,1,98304]{2,1,0:T(1,128)}, u32[]{:S(2)}, u32[]{:S(2)}) %all-to-all-start) | async-done | bytes 786464 | tf_op jit(solution)/shard_map/all_to_all | solution.py:66
  132.4 5.0 %reduce.1 = f32[2,98304]{1,0:T(2,128)} reduce(f32[2,1,98304]{2,1,0:T(1,128)} %all-to-all-done, f32[]{:T(128)} %broadcast.36), dimensions={1}, to_apply=%all_to_all.11.reduce_sub_computation | reduce | bytes 1572868 | tf_op jit(solution)/shard_map/all_to_all | solution.py:66
  137.4 4.7 %reshape.67 = f32[1024,6,32]{2,1,0:T(8,128)} reshape(f32[2,98304]{1,0:T(2,128)} %reduce.1) | data formatting | bytes 1572864
  142.1 4.4 %copy.17 = f32[6,32,2,512]{3,2,1,0:T(2,128)} copy(f32[6,32,2,512]{1,0,3,2:T(8,128)} %bitcast.34) | data formatting | bytes 1572864 | tf_op jit(solution)/shard_map/all_to_all | solution.py:66
  146.5 1.7 abs_reduce_fusion.1
  148.2 1.3 copy.16
  149.7 1.6 copy.20
  151.2 59.8 %while.11 = (s32[]{:T(128)}, f32[16,1024]{1,0:T(8,128)S(1)}, s32[16]{0:T(128)S(1)}, f32[12,16384]{1,0:T(8,128)}, s32[]{:T(128)}, /*index=5*/s32[]{:T(128)}, s32[]{:T(128)}) while((s32[]{:T(128)}, f32[16,1024]{1,0:T(8,128)S(1)}, s32[16]{0:T(128)S(1)}, f32[12,16384]{1,0:T(8,128)}, s32[]{:T(128)}, /*index=5*/s32[]{:T(128)}, s32[]{:T(128)}) %tuple.31), condition=%wide.region_3.4_spmd, body=%wide.region_1.3_spmd.sunk | while | flops 441349 | bytes 159875 | solution.py:28
  151.2 0.6 dynamic_slice.20
  153.8 1.0 constant_dynamic-slice_fusion.3
  155.0 0.6 dynamic_slice.20
  157.5 1.0 constant_dynamic-slice_fusion.3
  158.7 0.6 dynamic_slice.20
  161.2 1.0 constant_dynamic-slice_fusion.3
  162.5 0.6 dynamic_slice.20
  165.0 1.0 constant_dynamic-slice_fusion.3
  166.2 0.6 dynamic_slice.20
  168.7 1.0 constant_dynamic-slice_fusion.3
  169.9 0.6 dynamic_slice.20
  172.5 1.0 constant_dynamic-slice_fusion.3
  173.7 0.6 dynamic_slice.20
  176.2 1.0 constant_dynamic-slice_fusion.3
  177.4 0.6 dynamic_slice.20
  179.9 1.0 constant_dynamic-slice_fusion.3
  181.2 0.6 dynamic_slice.20
  183.7 1.0 constant_dynamic-slice_fusion.3
  184.9 0.6 dynamic_slice.20
  187.4 1.0 constant_dynamic-slice_fusion.3
  188.6 0.6 dynamic_slice.20
  191.2 1.0 constant_dynamic-slice_fusion.3
  192.4 0.6 dynamic_slice.20
  194.9 1.0 constant_dynamic-slice_fusion.3
  196.1 0.6 dynamic_slice.20
  198.6 1.0 constant_dynamic-slice_fusion.3
  199.9 0.6 dynamic_slice.20
  202.4 1.0 constant_dynamic-slice_fusion.3
  203.6 0.6 dynamic_slice.20
  206.1 1.0 constant_dynamic-slice_fusion.3
  207.3 0.6 dynamic_slice.20
  209.9 0.9 constant_dynamic-slice_fusion.3
  211.1 3.8 %all_gather.3 = f32[32,1024]{1,0:T(8,128)S(1)} all-gather(f32[32,512]{1,0:T(8,128)S(1)} %multiply_subtract_fusion), channel_id=1, replica_groups=mesh['dom'=16,'mem'=2] {'mem'}, dimensions={1}, use_global_device_ids=true | all-gather | bytes 196608 | tf_op jit(solution)/shard_map/all_gather | solution.py:74
  214.9 0.7 copy.34
  (55 shorter events, 4.8 us)
Async XLA Ops:
  0.0 10.7 %copy-start = (bf16[96,128,128]{2,1,0:T(8,128)(2,1)S(1)}, bf16[96,128,128]{2,1,0:T(8,128)(2,1)}, u32[]{:S(2)}) copy-start(bf16[96,128,128]{2,1,0:T(8,128)(2,1)} %param.10) | copy-start | bytes 9437188
  0.0 5.8 %copy-start.2 = (s32[96]{0:T(128)S(1)}, s32[96]{0:T(128)}, u32[]{:S(2)}) copy-start(s32[96]{0:T(128)} %param.12) | copy-start | bytes 1156
  24.5 21.3 %collective-permute-start = (f32[8,24576]{1,0:T(8,128)S(1)}, f32[8,24576]{1,0:T(8,128)S(1)}, u32[]{:S(2)}, u32[]{:S(2)}) collective-permute-start(f32[8,24576]{1,0:T(8,128)S(1)} %get-tuple-element.50), channel_id=1, source_target_pairs={{8,0},{10,2},{12,4},{14,6},{16,8},{18,10},{20,12},{22,14},{24,16},... | collective-permute-start | bytes 2359304 | tf_op jit(solution)/shard_map/ppermute | solution.py:13
  25.8 38.2 %collective-permute-start.1 = (f32[8,24576]{1,0:T(8,128)S(1)}, f32[8,24576]{1,0:T(8,128)S(1)}, u32[]{:S(2)}, u32[]{:S(2)}) collective-permute-start(f32[8,24576]{1,0:T(8,128)S(1)} %get-tuple-element.57), channel_id=1, source_target_pairs={{6,0},{8,2},{10,4},{12,6},{14,8},{16,10},{18,12},{20,14},{22,16},{... | collective-permute-start | bytes 2359304 | tf_op jit(solution)/shard_map/ppermute | solution.py:13
  27.1 49.9 %collective-permute-start.2 = (f32[8,24576]{1,0:T(8,128)S(1)}, f32[8,24576]{1,0:T(8,128)S(1)}, u32[]{:S(2)}, u32[]{:S(2)}) collective-permute-start(f32[8,24576]{1,0:T(8,128)S(1)} %get-tuple-element.56), channel_id=1, source_target_pairs={{4,0},{6,2},{8,4},{10,6},{12,8},{14,10},{16,12},{18,14},{20,16},{2... | collective-permute-start | bytes 2359304 | tf_op jit(solution)/shard_map/ppermute | solution.py:13
  28.4 72.2 %collective-permute-start.3 = (f32[8,24576]{1,0:T(8,128)S(1)}, f32[8,24576]{1,0:T(8,128)S(1)}, u32[]{:S(2)}, u32[]{:S(2)}) collective-permute-start(f32[8,24576]{1,0:T(8,128)S(1)} %get-tuple-element.55), channel_id=1, source_target_pairs={{2,0},{4,2},{6,4},{8,6},{10,8},{12,10},{14,12},{16,14},{18,16},{20... | collective-permute-start | bytes 2359304 | tf_op jit(solution)/shard_map/ppermute | solution.py:13
  30.4 70.2 %collective-permute-start.4 = (f32[8,24576]{1,0:T(8,128)S(1)}, f32[8,24576]{1,0:T(8,128)S(1)}, u32[]{:S(2)}, u32[]{:S(2)}) collective-permute-start(f32[8,24576]{1,0:T(8,128)S(1)} %get-tuple-element.54), channel_id=1, source_target_pairs={{0,2},{2,4},{4,6},{6,8},{8,10},{10,12},{12,14},{14,16},{16,18},{18... | collective-permute-start | bytes 2359304 | tf_op jit(solution)/shard_map/ppermute | solution.py:13
  45.8 54.8 %collective-permute-start.5 = (f32[8,24576]{1,0:T(8,128)S(1)}, f32[8,24576]{1,0:T(8,128)S(1)}, u32[]{:S(2)}, u32[]{:S(2)}) collective-permute-start(f32[8,24576]{1,0:T(8,128)S(1)} %get-tuple-element.53), channel_id=1, source_target_pairs={{0,4},{2,6},{4,8},{6,10},{8,12},{10,14},{12,16},{14,18},{16,20},{1... | collective-permute-start | bytes 2359304 | tf_op jit(solution)/shard_map/ppermute | solution.py:13
  64.1 36.6 %collective-permute-start.6 = (f32[8,24576]{1,0:T(8,128)S(1)}, f32[8,24576]{1,0:T(8,128)S(1)}, u32[]{:S(2)}, u32[]{:S(2)}) collective-permute-start(f32[8,24576]{1,0:T(8,128)S(1)} %get-tuple-element.52), channel_id=1, source_target_pairs={{0,6},{2,8},{4,10},{6,12},{8,14},{10,16},{12,18},{14,20},{16,22},{... | collective-permute-start | bytes 2359304 | tf_op jit(solution)/shard_map/ppermute | solution.py:13
  77.0 32.5 %collective-permute-start.7 = (f32[8,24576]{1,0:T(8,128)S(1)}, f32[8,24576]{1,0:T(8,128)S(1)}, u32[]{:S(2)}, u32[]{:S(2)}) collective-permute-start(f32[8,24576]{1,0:T(8,128)S(1)} %get-tuple-element.51), channel_id=1, source_target_pairs={{0,8},{2,10},{4,12},{6,14},{8,16},{10,18},{12,20},{14,22},{16,24},... | collective-permute-start | bytes 2359304 | tf_op jit(solution)/shard_map/ppermute | solution.py:13
  110.7 12.6 %copy-start.1 = (f32[32,1024]{1,0:T(8,128)S(1)}, f32[32,1024]{1,0:T(8,128)}, u32[]{:S(2)}) copy-start(f32[32,1024]{1,0:T(8,128)} %param.9) | copy-start | bytes 393220
  119.0 12.9 %all-to-all-start = ((f32[2,1,98304]{2,1,0:T(1,128)}), f32[2,1,98304]{2,1,0:T(1,128)}, u32[]{:S(2)}, u32[]{:S(2)}) async-start(f32[2,1,98304]{2,1,0:T(1,128)} %reshape.66), calls=%async_computation | async-start | bytes 1572864 | tf_op jit(solution)/shard_map/all_to_all | solution.py:66
where the time goes:
time: 217 us; the launch traced here: 216 us
  local copies, waits for them, and re-layouts  57.4 us (26%)
  starting transfers between devices  54.8 us (25%)
  waiting for transfers between devices  42.8 us (20%)
  loops' own time  31 us (14%)
  matrix products  13.4 us (6%)
  other arithmetic  11.4 us (5%)
  blocking collectives  3.78 us (2%)
    ppermute x8, starting transfers between devices, from_behind(): lax.ppermute(value, axis, [(source, source + steps) for source in range(f...  50.5 us
    ppermute x8, waiting for transfers between devices, from_behind(): lax.ppermute(value, axis, [(source, source + steps) for source in range(f...  34.4 us
    another operation x1, loops' own time, pair_total(): return lax.map(block_pairs, column_starts).reshape(left_set.shape[1:])  31 us
    dynamic_slice x16, local copies, waits for them, and re-layouts, block_pairs(): left_cols = lax.dynamic_slice_in_dim(flat_left, first_column, block_span, 1)  15.5 us
    unnamed x12, local copies, waits for them, and re-layouts  12.9 us
    dot_general x1, matrix products, on_device(): jnp.dot(chooser, partial_value.reshape(tile_slots, channels * block_cells...  10 us
    dynamic_slice x16, local copies, waits for them, and re-layouts, pair_total(): return lax.map(block_pairs, column_starts).reshape(left_set.shape[1:])  9.73 us
    all_to_all x1, waiting for transfers between devices, on_device(): lax.all_to_all(remapped, 'mem', split_axis=2, concat_axis=0, tiled=True)  8.48 us
  transfers between devices with their start and end apart: 9, of which 4 were waited for; matrix products, arithmetic and copies ran while one was open for 0% of the time, Pallas kernels for 0%

commit v1 on v0

--- a/solution.py
+++ b/solution.py
@@ -63,7 +63,10 @@
     )
     members = groups * lax.axis_size("mem")
     norm_pairs = 2.0 * members * (members - 1)
-    regrouped = lax.all_to_all(remapped, "mem", split_axis=2, concat_axis=0, tiled=True)
+    regrouped = jnp.concatenate(
+        lax.all_to_all(jnp.stack(jnp.split(remapped, lax.axis_size("mem"), axis=2)), "mem", 0, 0),
+        axis=0,
+    )
     part_cells = regrouped.shape[2]
     observed_part = lax.dynamic_slice_in_dim(
         observed, lax.axis_index("mem") * part_cells, part_cells, 1

time: 217 us -> 199 us (0.917)
  local copies, waits for them, and re-layouts: 57.4 us -> 43.4 us
  other arithmetic: 11.4 us -> 6.89 us
    unnamed x12 -> x10, local copies, waits for them, and re-layouts: 12.9 us -> 5.25 us
    all_to_all x3 -> x0, local copies, waits for them, and re-layouts: 6.29 us -> none  [on_device(): lax.all_to_all(remapped, 'mem', split_axis=2, concat_axis=0, tiled=True)]
    all_to_all x1 -> x0, other arithmetic: 4.98 us -> none  [on_device(): lax.all_to_all(remapped, 'mem', split_axis=2, concat_axis=0, tiled=True)]
    transpose x1 -> x0, local copies, waits for them, and re-layouts: 4.26 us -> none  [on_device(): remapped = summed.reshape(owned, groups, levels, block_cells).transpose(1...]
    reshape x0 -> x1, local copies, waits for them, and re-layouts: none -> 2.21 us  [on_device(): remapped = summed.reshape(owned, groups, levels, block_cells).transpose(1...]
where the time goes in v1:
time: 199 us; the launch traced here: 197 us
  starting transfers between devices  54.8 us (28%)
  local copies, waits for them, and re-layouts  43.4 us (22%)
  waiting for transfers between devices  42.9 us (22%)
  loops' own time  31 us (16%)
  matrix products  13.4 us (7%)
  other arithmetic  6.89 us (3%)
  blocking collectives  3.78 us (2%)
    ppermute x8, starting transfers between devices, from_behind(): lax.ppermute(value, axis, [(source, source + steps) for source in range(f...  50.5 us
    ppermute x8, waiting for transfers between devices, from_behind(): lax.ppermute(value, axis, [(source, source + steps) for source in range(f...  34.4 us
    another operation x1, loops' own time, pair_total(): return lax.map(block_pairs, column_starts).reshape(left_set.shape[1:])  31 us
    dynamic_slice x16, local copies, waits for them, and re-layouts, block_pairs(): left_cols = lax.dynamic_slice_in_dim(flat_left, first_column, block_span, 1)  15.5 us
    dynamic_slice x16, local copies, waits for them, and re-layouts, pair_total(): return lax.map(block_pairs, column_starts).reshape(left_set.shape[1:])  10.4 us
    dot_general x1, matrix products, on_device(): jnp.dot(chooser, partial_value.reshape(tile_slots, channels * block_cells...  10 us
    all_to_all x1, waiting for transfers between devices, on_device(): lax.all_to_all(jnp.stack(jnp.split(remapped, lax.axis_size('mem'), axis=2...  8.49 us
    unnamed x10, local copies, waits for them, and re-layouts  5.25 us
  transfers between devices with their start and end apart: 9, of which 4 were waited for; matrix products, arithmetic and copies ran while one was open for 0% of the time, Pallas kernels for 0%

profile of v1, /device:TPU:1, one launch (start us, length us, event | category | flops | bytes accessed | tf_op | source)
XLA Modules:
  0.0 197.0 jit_solution(6682831891145494302)
XLA Ops:
  0.0 0.8 compare_select_fusion
  0.8 0.8 compare_and_fusion
  1.6 1.7 copy.9
  3.4 1.8 copy.8
  5.9 4.9 %gather_fusion = bf16[96,192,128]{2,1,0:T(8,128)(2,1)} fusion(bf16[192,32,128]{2,0,1:T(8,128)(2,1)} %copy.8, s32[1024]{0:T(1024)S(1)} %pad_clamp_fusion), kind=kCustom, calls=%fused_computation | custom fusion | bytes 9437568 | tf_op jit(solution)/shard_map/jit(_take)/gather | solution.py:37
  10.7 3.4 %fusion.3 = f32[96,192,128]{2,1,0:T(8,128)S(1)} fusion(bf16[96,128,128]{2,1,0:T(8,128)(2,1)S(1)} %copy-done, bf16[96,192,128]{2,1,0:T(8,128)(2,1)} %gather_fusion, pred[96]{0:T(512)(128)(4,1)S(1)} %compare_and_fusion), kind=kOutput, calls=%fused_computation.6 | convolution fusion | flops 606339072 | bytes 17301600 | tf_op jit(solution)/shard_map/csi,sij->scj/dot_general | solution.py:38
  14.1 10.0 %fusion = f32[72,24576]{1,0:T(8,128)S(1)} fusion(f32[12,8,192,128]{3,2,1,0:T(8,128)S(1)} %bitcast.32, s32[96]{0:T(128)S(1)} %broadcast_subtract_fusion, pred[96]{0:T(512)(128)(4,1)S(1)} %iota_compare_fusion.1), kind=kOutput, calls=%fused_computation.3 | convolution fusion | flops 2038445568 | bytes 16515552 | tf_op jit(solution)/shard_map/dot_general | solution.py:48
  24.2 0.4 fusion.20
  24.6 1.3 collective-permute-start
  25.9 1.3 collective-permute-start.1
  27.2 1.3 collective-permute-start.2
  28.5 1.9 collective-permute-start.3
  30.4 5.1 %collective-permute-start.4 = (f32[8,24576]{1,0:T(8,128)S(1)}, f32[8,24576]{1,0:T(8,128)S(1)}, u32[]{:S(2)}, u32[]{:S(2)}) collective-permute-start(f32[8,24576]{1,0:T(8,128)S(1)} %get-tuple-element.54), channel_id=1, source_target_pairs={{0,2},{2,4},{4,6},{6,8},{8,10},{10,12},{12,14},{14,16},{16,18},{18... | collective-permute-start | bytes 2359304 | tf_op jit(solution)/shard_map/ppermute | solution.py:13
  35.5 10.3 %collective-permute-done = f32[8,24576]{1,0:T(8,128)S(1)} collective-permute-done((f32[8,24576]{1,0:T(8,128)S(1)}, f32[8,24576]{1,0:T(8,128)S(1)}, u32[]{:S(2)}, u32[]{:S(2)}) %collective-permute-start) | collective-permute-done | bytes 786464 | tf_op jit(solution)/shard_map/ppermute | solution.py:13
  45.8 3.0 %collective-permute-start.5 = (f32[8,24576]{1,0:T(8,128)S(1)}, f32[8,24576]{1,0:T(8,128)S(1)}, u32[]{:S(2)}, u32[]{:S(2)}) collective-permute-start(f32[8,24576]{1,0:T(8,128)S(1)} %get-tuple-element.53), channel_id=1, source_target_pairs={{0,4},{2,6},{4,8},{6,10},{8,12},{10,14},{12,16},{14,18},{16,20},{1... | collective-permute-start | bytes 2359304 | tf_op jit(solution)/shard_map/ppermute | solution.py:13
  48.9 15.2 %collective-permute-done.1 = f32[8,24576]{1,0:T(8,128)S(1)} collective-permute-done((f32[8,24576]{1,0:T(8,128)S(1)}, f32[8,24576]{1,0:T(8,128)S(1)}, u32[]{:S(2)}, u32[]{:S(2)}) %collective-permute-start.1) | collective-permute-done | bytes 786464 | tf_op jit(solution)/shard_map/ppermute | solution.py:13
  64.1 12.7 %collective-permute-start.6 = (f32[8,24576]{1,0:T(8,128)S(1)}, f32[8,24576]{1,0:T(8,128)S(1)}, u32[]{:S(2)}, u32[]{:S(2)}) collective-permute-start(f32[8,24576]{1,0:T(8,128)S(1)} %get-tuple-element.52), channel_id=1, source_target_pairs={{0,6},{2,8},{4,10},{6,12},{8,14},{10,16},{12,18},{14,20},{16,22},{... | collective-permute-start | bytes 2359304 | tf_op jit(solution)/shard_map/ppermute | solution.py:13
  76.9 23.8 %collective-permute-start.7 = (f32[8,24576]{1,0:T(8,128)S(1)}, f32[8,24576]{1,0:T(8,128)S(1)}, u32[]{:S(2)}, u32[]{:S(2)}) collective-permute-start(f32[8,24576]{1,0:T(8,128)S(1)} %get-tuple-element.51), channel_id=1, source_target_pairs={{0,8},{2,10},{4,12},{6,14},{8,16},{10,18},{12,20},{14,22},{16,24},... | collective-permute-start | bytes 2359304 | tf_op jit(solution)/shard_map/ppermute | solution.py:13
  100.7 8.8 %collective-permute-done.7 = f32[8,24576]{1,0:T(8,128)S(1)} collective-permute-done((f32[8,24576]{1,0:T(8,128)S(1)}, f32[8,24576]{1,0:T(8,128)S(1)}, u32[]{:S(2)}, u32[]{:S(2)}) %collective-permute-start.7) | collective-permute-done | bytes 786464 | tf_op jit(solution)/shard_map/ppermute | solution.py:13
  109.5 1.2 fusion.14
  110.7 2.2 %reshape.51 = f32[6,32,1024]{2,1,0:T(8,128)} reshape(f32[6,32,8,128]{3,2,1,0:T(8,128)} %bitcast.35) | data formatting | bytes 1572864 | tf_op jit(solution)/shard_map/reshape | solution.py:62
  112.9 1.2 slice_bitcast_fusion.1
  114.1 1.0 pad_maximum_fusion
  115.1 4.3 %all-to-all-start = ((f32[2,6,32,512]{3,2,1,0:T(8,128)}), f32[2,6,32,512]{3,2,1,0:T(8,128)}, u32[]{:S(2)}, u32[]{:S(2)}) async-start(f32[2,6,32,512]{3,2,1,0:T(8,128)} %pad_maximum_fusion), calls=%async_computation | async-start | bytes 1572864 | tf_op jit(solution)/shard_map/all_to_all | solution.py:67
  119.5 8.5 %all-to-all-done = f32[2,6,32,512]{3,2,1,0:T(8,128)} async-done(((f32[2,6,32,512]{3,2,1,0:T(8,128)}), f32[2,6,32,512]{3,2,1,0:T(8,128)}, u32[]{:S(2)}, u32[]{:S(2)}) %all-to-all-start) | async-done | bytes 786464 | tf_op jit(solution)/shard_map/all_to_all | solution.py:67
  127.9 1.2 pad.3
  129.2 1.6 copy.11
  130.8 60.5 %while.11 = (s32[]{:T(128)}, f32[16,1024]{1,0:T(8,128)S(1)}, s32[16]{0:T(128)S(1)}, f32[12,16384]{1,0:T(8,128)}, s32[]{:T(128)}, /*index=5*/s32[]{:T(128)}, s32[]{:T(128)}) while((s32[]{:T(128)}, f32[16,1024]{1,0:T(8,128)S(1)}, s32[16]{0:T(128)S(1)}, f32[12,16384]{1,0:T(8,128)}, s32[]{:T(128)}, /*index=5*/s32[]{:T(128)}, s32[]{:T(128)}) %tuple.32), condition=%wide.region_3.4_spmd, body=%wide.region_1.3_spmd.sunk | while | flops 441349 | bytes 159875 | solution.py:28
  130.8 0.6 dynamic_slice.20
  133.3 1.0 constant_dynamic-slice_fusion.3
  134.6 0.7 dynamic_slice.20
  137.1 1.0 constant_dynamic-slice_fusion.3
  138.4 0.7 dynamic_slice.20
  140.9 1.0 constant_dynamic-slice_fusion.3
  142.1 0.7 dynamic_slice.20
  144.7 1.0 constant_dynamic-slice_fusion.3
  145.9 0.7 dynamic_slice.20
  148.5 1.0 constant_dynamic-slice_fusion.3
  149.7 0.7 dynamic_slice.20
  152.3 1.0 constant_dynamic-slice_fusion.3
  153.2 0.1 abs_reduce_fusion.3
  153.5 0.7 dynamic_slice.20
  156.0 1.0 constant_dynamic-slice_fusion.3
  157.3 0.7 dynamic_slice.20
  159.8 1.0 constant_dynamic-slice_fusion.3
  161.1 0.7 dynamic_slice.20
  163.6 1.0 constant_dynamic-slice_fusion.3
  164.8 0.7 dynamic_slice.20
  167.4 1.0 constant_dynamic-slice_fusion.3
  168.6 0.7 dynamic_slice.20
  171.2 1.0 constant_dynamic-slice_fusion.3
  172.4 0.7 dynamic_slice.20
  175.0 1.0 constant_dynamic-slice_fusion.3
  176.2 0.7 dynamic_slice.20
  178.7 1.0 constant_dynamic-slice_fusion.3
  180.0 0.7 dynamic_slice.20
  182.5 1.0 constant_dynamic-slice_fusion.3
  183.7 0.7 dynamic_slice.20
  186.3 1.0 constant_dynamic-slice_fusion.3
  187.5 0.7 dynamic_slice.20
  190.1 0.9 constant_dynamic-slice_fusion.3
  191.3 1.2 abs_reduce_fusion.1
  192.6 3.8 %all_gather.3 = f32[32,1024]{1,0:T(8,128)S(1)} all-gather(f32[32,512]{1,0:T(8,128)S(1)} %multiply_subtract_fusion), channel_id=1, replica_groups=mesh['dom'=16,'mem'=2] {'mem'}, dimensions={1}, use_global_device_ids=true | all-gather | bytes 196608 | tf_op jit(solution)/shard_map/all_gather | solution.py:77
  196.3 0.7 copy.25
  (51 shorter events, 3.6 us)
Async XLA Ops:
  0.0 10.7 %copy-start = (bf16[96,128,128]{2,1,0:T(8,128)(2,1)S(1)}, bf16[96,128,128]{2,1,0:T(8,128)(2,1)}, u32[]{:S(2)}) copy-start(bf16[96,128,128]{2,1,0:T(8,128)(2,1)} %param.10) | copy-start | bytes 9437188
  0.0 5.8 %copy-start.2 = (s32[96]{0:T(128)S(1)}, s32[96]{0:T(128)}, u32[]{:S(2)}) copy-start(s32[96]{0:T(128)} %param.12) | copy-start | bytes 1156
  24.6 21.3 %collective-permute-start = (f32[8,24576]{1,0:T(8,128)S(1)}, f32[8,24576]{1,0:T(8,128)S(1)}, u32[]{:S(2)}, u32[]{:S(2)}) collective-permute-start(f32[8,24576]{1,0:T(8,128)S(1)} %get-tuple-element.50), channel_id=1, source_target_pairs={{8,0},{10,2},{12,4},{14,6},{16,8},{18,10},{20,12},{22,14},{24,16},... | collective-permute-start | bytes 2359304 | tf_op jit(solution)/shard_map/ppermute | solution.py:13
  25.9 38.2 %collective-permute-start.1 = (f32[8,24576]{1,0:T(8,128)S(1)}, f32[8,24576]{1,0:T(8,128)S(1)}, u32[]{:S(2)}, u32[]{:S(2)}) collective-permute-start(f32[8,24576]{1,0:T(8,128)S(1)} %get-tuple-element.57), channel_id=1, source_target_pairs={{6,0},{8,2},{10,4},{12,6},{14,8},{16,10},{18,12},{20,14},{22,16},{... | collective-permute-start | bytes 2359304 | tf_op jit(solution)/shard_map/ppermute | solution.py:13
  27.2 49.7 %collective-permute-start.2 = (f32[8,24576]{1,0:T(8,128)S(1)}, f32[8,24576]{1,0:T(8,128)S(1)}, u32[]{:S(2)}, u32[]{:S(2)}) collective-permute-start(f32[8,24576]{1,0:T(8,128)S(1)} %get-tuple-element.56), channel_id=1, source_target_pairs={{4,0},{6,2},{8,4},{10,6},{12,8},{14,10},{16,12},{18,14},{20,16},{2... | collective-permute-start | bytes 2359304 | tf_op jit(solution)/shard_map/ppermute | solution.py:13
  28.5 72.2 %collective-permute-start.3 = (f32[8,24576]{1,0:T(8,128)S(1)}, f32[8,24576]{1,0:T(8,128)S(1)}, u32[]{:S(2)}, u32[]{:S(2)}) collective-permute-start(f32[8,24576]{1,0:T(8,128)S(1)} %get-tuple-element.55), channel_id=1, source_target_pairs={{2,0},{4,2},{6,4},{8,6},{10,8},{12,10},{14,12},{16,14},{18,16},{20... | collective-permute-start | bytes 2359304 | tf_op jit(solution)/shard_map/ppermute | solution.py:13
  30.4 70.2 %collective-permute-start.4 = (f32[8,24576]{1,0:T(8,128)S(1)}, f32[8,24576]{1,0:T(8,128)S(1)}, u32[]{:S(2)}, u32[]{:S(2)}) collective-permute-start(f32[8,24576]{1,0:T(8,128)S(1)} %get-tuple-element.54), channel_id=1, source_target_pairs={{0,2},{2,4},{4,6},{6,8},{8,10},{10,12},{12,14},{14,16},{16,18},{18... | collective-permute-start | bytes 2359304 | tf_op jit(solution)/shard_map/ppermute | solution.py:13
  45.8 54.8 %collective-permute-start.5 = (f32[8,24576]{1,0:T(8,128)S(1)}, f32[8,24576]{1,0:T(8,128)S(1)}, u32[]{:S(2)}, u32[]{:S(2)}) collective-permute-start(f32[8,24576]{1,0:T(8,128)S(1)} %get-tuple-element.53), channel_id=1, source_target_pairs={{0,4},{2,6},{4,8},{6,10},{8,12},{10,14},{12,16},{14,18},{16,20},{1... | collective-permute-start | bytes 2359304 | tf_op jit(solution)/shard_map/ppermute | solution.py:13
  64.1 36.6 %collective-permute-start.6 = (f32[8,24576]{1,0:T(8,128)S(1)}, f32[8,24576]{1,0:T(8,128)S(1)}, u32[]{:S(2)}, u32[]{:S(2)}) collective-permute-start(f32[8,24576]{1,0:T(8,128)S(1)} %get-tuple-element.52), channel_id=1, source_target_pairs={{0,6},{2,8},{4,10},{6,12},{8,14},{10,16},{12,18},{14,20},{16,22},{... | collective-permute-start | bytes 2359304 | tf_op jit(solution)/shard_map/ppermute | solution.py:13
  76.9 32.6 %collective-permute-start.7 = (f32[8,24576]{1,0:T(8,128)S(1)}, f32[8,24576]{1,0:T(8,128)S(1)}, u32[]{:S(2)}, u32[]{:S(2)}) collective-permute-start(f32[8,24576]{1,0:T(8,128)S(1)} %get-tuple-element.51), channel_id=1, source_target_pairs={{0,8},{2,10},{4,12},{6,14},{8,16},{10,18},{12,20},{14,22},{16,24},... | collective-permute-start | bytes 2359304 | tf_op jit(solution)/shard_map/ppermute | solution.py:13
  110.7 8.7 %copy-start.1 = (f32[32,1024]{1,0:T(8,128)S(1)}, f32[32,1024]{1,0:T(8,128)}, u32[]{:S(2)}) copy-start(f32[32,1024]{1,0:T(8,128)} %param.9) | copy-start | bytes 393220
  115.1 12.9 %all-to-all-start = ((f32[2,6,32,512]{3,2,1,0:T(8,128)}), f32[2,6,32,512]{3,2,1,0:T(8,128)}, u32[]{:S(2)}, u32[]{:S(2)}) async-start(f32[2,6,32,512]{3,2,1,0:T(8,128)} %pad_maximum_fusion), calls=%async_computation | async-start | bytes 1572864 | tf_op jit(solution)/shard_map/all_to_all | solution.py:67
